TPU v7x, 32 devices: a whole 2x2x4 slice. The times are simulated.
32 devices in a mesh: ctx: 8 (over z, core), tp: 4 (over y, x).
Axes of the slice: x: 2, y: 2, z: 4, core: 2. Of those that a mesh axis runs over, the one named last changes fastest.
Arguments:
- tokens: bfloat16 [4096, 4096], P(('ctx', 'tp')), may hold values from -6 to 6
- in_weight: bfloat16 [3, 4096, 2048], P(None, None, 'tp'), may hold values from -0.09375 to 0.09375
- short_taps: float32 [3, 3, 2048], P(None, None, 'tp'), may hold values from -3 to 3
- decay_rate: float32 [16, 2048], P(None, 'tp'), may hold values from 4.8828125e-05 to 0.0333333333
- residue: float32 [16, 2048], P(None, 'tp'), may hold values from -0.26 to 0.26
- skip_gain: float32 [2048], P('tp'), may hold values from -4 to 4
- grad_out: bfloat16 [4096, 2048], P('ctx', 'tp'), may hold values from -6 to 6
Outputs:
- mixed_out: bfloat16 [4096, 2048], P('ctx', 'tp')
- input_grad: bfloat16 [4096, 4096], P(('ctx', 'tp'))
All inputs are finite; a program needn't handle non-finite values.
Results may differ from a plain program's by a relative error of at most 0.0065.
Values may be sent and summed in bfloat16 or wider, within the bound.
A program may use at most 192 MiB of HBM per device.

v0:
```python
import jax
import jax.numpy as jnp
from jax import lax
from jax.sharding import PartitionSpec as P

exact_mode = lax.Precision.HIGHEST


def from_behind(value, axis, steps):
    count = lax.axis_size(axis)
    leading, last = (max(0, -steps), min(count, count - steps))
    return lax.ppermute(value, axis, [(source, source + steps) for source in range(leading, last)])


def modal_block(signal, log_pole, residue):
    length, channels = signal.shape
    sub_len = min(64, length)
    sub_count = length // sub_len
    offsets = jnp.arange(sub_len, dtype=jnp.float32)
    sections = signal.reshape(sub_count, sub_len, channels)
    powers = jnp.exp(log_pole[:, None, :] * offsets[None, :, None])
    filter_taps = jnp.sum(residue[:, None, :] * powers, axis=0)
    lag_index = jnp.arange(sub_len)[:, None] - jnp.arange(sub_len)[None, :]
    toeplitz = jnp.where((lag_index >= 0)[:, :, None], filter_taps[jnp.maximum(lag_index, 0)], 0.0)
    within = jnp.einsum("abc,kbc->kac", toeplitz, sections, precision=exact_mode)
    to_end = jnp.exp(log_pole[:, None, :] * (sub_len - 1.0 - offsets)[None, :, None])
    end_states = jnp.einsum("nbc,kbc->nkc", to_end, sections, precision=exact_mode)
    lag_blocks = jnp.arange(sub_count + 1)[:, None] - 1 - jnp.arange(sub_count)[None, :]
    valid_lag = lag_blocks >= 0
    lag_float = (jnp.maximum(lag_blocks, 0) * sub_len).astype(jnp.float32)
    decay_table = jnp.exp(log_pole[None, None] * lag_float[:, :, None, None])
    decay_table = jnp.where(valid_lag[:, :, None, None], decay_table, 0.0)
    carried = jnp.einsum("kmnc,nmc->nkc", decay_table, end_states, precision=exact_mode)
    stepped = residue[:, None, :] * jnp.exp(log_pole[:, None, :] * (offsets[None, :, None] + 1.0))
    output = within + jnp.einsum(
        "nac,nkc->kac", stepped, carried[:, :sub_count], precision=exact_mode
    )
    return (output.reshape(length, channels), carried[:, sub_count])


def carry_term(incoming, log_pole, residue, length):
    channels = incoming.shape[1]
    sub_len = min(64, length)
    sub_count = length // sub_len
    offsets = jnp.arange(sub_len, dtype=jnp.float32)
    stepped = residue[:, None, :] * jnp.exp(log_pole[:, None, :] * (offsets[None, :, None] + 1.0))
    block_starts = (jnp.arange(sub_count) * sub_len).astype(jnp.float32)
    start_states = incoming[:, None, :] * jnp.exp(
        log_pole[:, None, :] * block_starts[None, :, None]
    )
    output = jnp.einsum("nac,nkc->kac", stepped, start_states, precision=exact_mode)
    return output.reshape(length, channels)


def shards(tokens, in_weight, short_taps, decay_rate, residue, skip_gain, grad_out):
    width = in_weight.shape[2]
    weight_cat = jnp.concatenate([in_weight[0], in_weight[1], in_weight[2]], axis=1)
    streams = jnp.dot(
        lax.all_gather(tokens, "tp", axis=0, tiled=True),
        weight_cat,
        preferred_element_type=jnp.float32,
    ).astype(jnp.bfloat16)
    length = streams.shape[0]
    tap_reach = short_taps.shape[1] - 1
    taps_cat = jnp.concatenate([short_taps[0], short_taps[1], short_taps[2]], axis=1)
    before = from_behind(streams[length - tap_reach :], "ctx", 1)
    extended = jnp.concatenate([before, streams], axis=0).astype(jnp.float32)
    short_mixed = taps_cat[0][None] * extended[tap_reach:]
    for offset in range(1, tap_reach + 1):
        short_mixed = (
            short_mixed
            + taps_cat[offset][None] * extended[tap_reach - offset : tap_reach - offset + length]
        )
    query_side = short_mixed[:, :width]
    key_side = short_mixed[:, width : 2 * width]
    value_side = short_mixed[:, 2 * width :]
    product_in = key_side * value_side
    log_pole = -decay_rate
    forward_local, forward_sum = modal_block(product_in, log_pole, residue)
    upstream = grad_out.astype(jnp.float32)
    conv_grad = upstream * query_side
    backward_local, backward_sum = modal_block(conv_grad[::-1], log_pole, residue)
    position = lax.axis_index("ctx")
    summaries = (
        lax.all_gather(forward_sum[None], "ctx", axis=0, tiled=True),
        lax.all_gather(backward_sum[None], "ctx", axis=0, tiled=True),
    )
    block_index = jnp.arange(summaries[0].shape[0])
    earlier_gap = position - 1 - block_index
    later_gap = block_index - position - 1
    scale_fwd = (jnp.maximum(earlier_gap, 0) * length).astype(jnp.float32)
    scale_bwd = (jnp.maximum(later_gap, 0) * length).astype(jnp.float32)
    weight_fwd = jnp.where(
        (earlier_gap >= 0)[:, None, None], jnp.exp(log_pole[None] * scale_fwd[:, None, None]), 0.0
    )
    weight_bwd = jnp.where(
        (later_gap >= 0)[:, None, None], jnp.exp(log_pole[None] * scale_bwd[:, None, None]), 0.0
    )
    incoming_fwd = jnp.sum(weight_fwd * summaries[0], axis=0)
    incoming_bwd = jnp.sum(weight_bwd * summaries[1], axis=0)
    conv_out = forward_local + carry_term(incoming_fwd, log_pole, residue, length)
    back_conv = (backward_local + carry_term(incoming_bwd, log_pole, residue, length))[::-1]
    filtered = conv_out + skip_gain[None] * product_in
    result = (query_side * filtered).astype(jnp.bfloat16)
    grad_query = upstream * filtered
    grad_product = back_conv + skip_gain[None] * conv_grad
    stream_grads = jnp.concatenate(
        [grad_query, grad_product * value_side, grad_product * key_side], axis=1
    )
    after_rows = from_behind(stream_grads[:tap_reach], "ctx", -1)
    padded = jnp.concatenate([stream_grads, after_rows], axis=0)
    grad_streams = taps_cat[0][None] * padded[:length]
    for offset in range(1, tap_reach + 1):
        grad_streams = grad_streams + taps_cat[offset][None] * padded[offset : offset + length]
    grad_streams = grad_streams.astype(jnp.bfloat16)
    input_grad = lax.psum_scatter(
        jnp.einsum("rk,dk->rd", grad_streams, weight_cat, preferred_element_type=jnp.float32),
        "tp",
        scatter_dimension=0,
        tiled=True,
    )
    return (result, input_grad.astype(jnp.bfloat16))


def solution(mesh):
    in_specs = (
        P(("ctx", "tp"), None),
        P(None, None, "tp"),
        P(None, None, "tp"),
        P(None, "tp"),
        P(None, "tp"),
        P("tp"),
        P("ctx", "tp"),
    )
    out_specs = (P("ctx", "tp"), P(("ctx", "tp"), None))
    return jax.shard_map(shards, mesh=mesh, in_specs=in_specs, out_specs=out_specs, check_vma=False)
```

profile of v0, /device:TPU:0, one launch (start us, length us, event | category | flops | bytes accessed | tf_op | source)
XLA Modules:
  0.0 425.8 jit_solution(13734944484443830677)
XLA Ops:
  10.8 6.0 %multiply_reduce_fusion = f32[64,512]{0,1:T(8,128)S(1)} fusion(f32[16,512]{0,1:T(8,128)S(1)} %copy.29, f32[16,512]{0,1:T(8,128)S(1)} %copy.28), kind=kLoop, calls=%fused_computation.20 | loop fusion | flops 1540096 | bytes 196608 | tf_op jit(solution)/shard_map/reduce_sum | solution.py:22
  16.8 10.3 %slice_bitcast_fusion.2 = (bf16[4096,512]{1,0:T(8,128)(2,1)}, bf16[4096,512]{1,0:T(8,128)(2,1)}, bf16[4096,512]{1,0:T(8,128)(2,1)}) fusion(bf16[3,4096,512]{2,1,0:T(8,128)(2,1)} %param.8), kind=kLoop, calls=%fused_computation.23 | loop fusion | bytes 25165824 | tf_op jit(solution)/shard_map/squeeze | solution.py:57
  27.1 38.0 %all-gather.4.cloned.1.call-done = bf16[512,4096]{1,0:T(8,128)(2,1)} async-done(((bf16[128,4096]{1,0:T(8,128)(2,1)}), bf16[512,4096]{1,0:T(8,128)(2,1)}) %all-gather.4.cloned.1.call-update) | async-done | bytes 4194320 | tf_op jit(solution)/shard_map/all_gather | solution.py:59
  65.1 12.5 %fusion.22 = bf16[512,1536]{1,0:T(8,128)(2,1)S(1)} fusion(bf16[512,4096]{1,0:T(8,128)(2,1)} %all-gather.4.cloned.1.call-done, bf16[4096,512]{1,0:T(8,128)(2,1)} %get-tuple-element.10, bf16[4096,512]{1,0:T(8,128)(2,1)} %get-tuple-element.11, bf16[4096,512]{1,0:T(8,128)(2,1)} %get-tuple-element.9), kind=kOutput, calls=%fused_computation.37 | convolution fusion | flops 6480986112 | bytes 18350080 | tf_op jit(solution)/shard_map/dot_general | solution.py:58
  79.5 16.8 %gather_fusion = f32[4096,512]{1,0:T(8,128)} fusion(f32[64,512]{1,0:T(8,128)S(1)} %copy.30, s32[4096]{0:T(1024)S(1)} %broadcast_clamp_fusion), kind=kCustom, calls=%fused_computation | custom fusion | bytes 16793600 | tf_op jit(solution)/shard_map/gather | solution.py:24
  96.4 16.3 %copy.31 = f32[64,64,512]{1,0,2:T(8,128)} copy(f32[64,64,512]{2,1,0:T(8,128)} %bitcast.51) | data formatting | bytes 16777216 | tf_op jit(solution)/shard_map/gather | solution.py:24
  116.0 8.9 %rev.6 = f32[512,512]{1,0:T(8,128)} reverse(f32[512,512]{1,0:T(8,128)} %get-tuple-element.15), dimensions={0} | reverse | bytes 2097152 | tf_op jit(solution)/shard_map/rev | solution.py:82
  131.2 9.5 %fusion.43 = f32[16,512,8]{0,2,1:T(8,128)} fusion(f32[8,64,512]{1,0,2:T(8,128)} %copy.32, f32[64]{0:T(128)S(1)} %iota_subtract_fusion.2, f32[16,512]{0,1:T(8,128)S(1)} %copy.29), kind=kOutput, calls=%fused_computation.64 | convolution fusion | flops 50855936 | bytes 1343744 | tf_op jit(solution)/shard_map/nbc,kbc->nkc/dot_general | solution.py:27
  140.7 30.2 %fusion.2 = f32[512,8,64]{2,1,0:T(8,128)} fusion(f32[8,64,512]{1,0,2:T(8,128)S(1)} %copy-done.1, f32[64,64,512]{1,0,2:T(8,128)} %copy.31, pred[64,64]{1,0:T(8,128)(4,1)S(1)} %subtract_compare_fusion), kind=kOutput, calls=%fused_computation.3 | convolution fusion | flops 203423744 | bytes 10489856 | tf_op jit(solution)/shard_map/abc,kbc->kac/dot_general | solution.py:25
  170.9 30.5 %fusion = f32[512,8,64]{2,1,0:T(8,128)} fusion(f32[8,64,512]{1,0,2:T(8,128)S(1)} %copy-done, f32[64,64,512]{1,0,2:T(8,128)} %copy.31, pred[64,64]{1,0:T(8,128)(4,1)S(1)} %subtract_compare_fusion), kind=kOutput, calls=%fused_computation.1 | convolution fusion | flops 203423744 | bytes 10489856 | tf_op jit(solution)/shard_map/abc,kbc->kac/dot_general | solution.py:25
  201.4 8.3 %fusion.44 = f32[16,512,8]{0,2,1:T(8,128)} fusion(f32[8,64,512]{1,0,2:T(8,128)S(1)} %copy-done, f32[64]{0:T(128)S(1)} %iota_subtract_fusion.2, f32[16,512]{0,1:T(8,128)S(1)} %copy.29), kind=kOutput, calls=%fused_computation.65 | convolution fusion | flops 50855936 | bytes 1343744 | tf_op jit(solution)/shard_map/nbc,kbc->nkc/dot_general | solution.py:27
  218.2 4.5 %copy.58 = f32[16,512,9]{0,2,1:T(8,128)} copy(f32[16,512,9]{1,0,2:T(8,128)} %get-tuple-element.2) | data formatting | bytes 589824 | tf_op jit(solution)/shard_map/kmnc,nmc->nkc/dot_general | solution.py:33
  226.2 14.7 %all-gather.1 = f32[128,1,512]{2,1,0:T(1,128)S(1)} all-gather(f32[16,1,512]{2,1,0:T(1,128)S(1)} %copy.40), channel_id=3, replica_groups=mesh['ctx'=8,'tp'=4] {'ctx'}, dimensions={0}, use_global_device_ids=true | all-gather | bytes 294912 | tf_op jit(solution)/shard_map/all_gather | solution.py:86
  241.6 4.5 %copy.50 = f32[16,512,9]{0,2,1:T(8,128)} copy(f32[16,512,9]{1,0,2:T(8,128)} %get-tuple-element.3) | data formatting | bytes 589824 | tf_op jit(solution)/shard_map/kmnc,nmc->nkc/dot_general | solution.py:33
  249.6 14.2 %all-gather = f32[128,1,512]{2,1,0:T(1,128)S(1)} all-gather(f32[16,1,512]{2,1,0:T(1,128)S(1)} %copy.34), channel_id=2, replica_groups=mesh['ctx'=8,'tp'=4] {'ctx'}, dimensions={0}, use_global_device_ids=true | all-gather | bytes 294912 | tf_op jit(solution)/shard_map/all_gather | solution.py:85
  266.6 6.7 %fusion.12 = f32[512,8,64]{2,1,0:T(8,128)S(1)} fusion(f32[64]{0:T(128)S(1)} %iota_add_fusion, f32[16,512]{0,1:T(8,128)S(1)} %copy.29, f32[16,512]{0,1:T(8,128)} %copy-done.9, f32[8]{0:T(128)S(1)} %multiply_convert_fusion.3, f32[16,512]{0,1:T(8,128)} %copy.35), kind=kOutput, calls=%fused_computation.15 | convolution fusion | flops 51511296 | bytes 1147168 | tf_op jit(solution)/shard_map/nac,nkc->kac/dot_general | solution.py:51
  273.3 6.5 %add_bitcast_fusion.1 = f32[8,64,512]{1,0,2:T(8,128)} fusion(f32[512,8,64]{2,1,0:T(8,128)S(1)} %fusion.12, f32[512,8,64]{2,1,0:T(8,128)S(1)} %copy-done.8, f32[64]{0:T(128)S(1)} %iota_add_fusion, f32[16,512]{0,1:T(8,128)S(1)} %copy.29, f32[16,512]{0,1:T(8,128)S(1)} %copy-done.10, f32[16,9,512]{0,1,2:T(8,128)S(1)} %bitcast.55), kind=kOutput, calls=%fused_computation.45 | convolution fusion | flops 51904512 | bytes 7864832 | tf_op jit(solution)/shard_map/nac,nkc->kac/dot_general | solution.py:35
  283.0 6.5 %fusion.10 = f32[512,8,64]{2,1,0:T(8,128)S(1)} fusion(f32[64]{0:T(128)S(1)} %iota_add_fusion, f32[16,512]{0,1:T(8,128)S(1)} %copy.29, f32[16,512]{0,1:T(8,128)} %copy-done.9, f32[16,512]{0,1:T(8,128)} %copy.41, f32[8]{0:T(128)S(1)} %multiply_convert_fusion.3), kind=kOutput, calls=%fused_computation.13 | convolution fusion | flops 51511296 | bytes 1147168 | tf_op jit(solution)/shard_map/nac,nkc->kac/dot_general | solution.py:51
  289.5 6.5 %add_bitcast_fusion = f32[8,64,512]{1,0,2:T(8,128)} fusion(f32[512,8,64]{2,1,0:T(8,128)S(1)} %fusion.10, f32[512,8,64]{2,1,0:T(8,128)S(1)} %copy-done.7, f32[64]{0:T(128)S(1)} %iota_add_fusion, f32[16,512]{0,1:T(8,128)S(1)} %copy.29, f32[16,512]{0,1:T(8,128)S(1)} %copy-done.11, f32[16,9,512]{0,1,2:T(8,128)S(1)} %bitcast.53), kind=kOutput, calls=%fused_computation.43 | convolution fusion | flops 51904512 | bytes 7864832 | tf_op jit(solution)/shard_map/nac,nkc->kac/dot_general | solution.py:35
  296.0 3.2 copy.42
  299.2 8.9 %rev.7 = f32[512,512]{1,0:T(8,128)} reverse(f32[512,512]{1,0:T(8,128)} %bitcast.57), dimensions={0} | reverse | bytes 2097152 | tf_op jit(solution)/shard_map/rev | solution.py:102
  308.2 4.1 slice_multiply_fusion.5
  315.8 13.3 %fusion.8 = f32[512,4096]{1,0:T(8,128)} fusion(bf16[4096,512]{1,0:T(8,128)(2,1)} %get-tuple-element.10, bf16[4096,512]{1,0:T(8,128)(2,1)} %get-tuple-element.11, bf16[4096,512]{1,0:T(8,128)(2,1)} %get-tuple-element.9, f32[514,1536]{1,0:T(8,128)S(1)} %pad_maximum_fusion.3, f32[1536]{0:T(1024)S(1)} %get-tuple-element.8, f32[1536]{0:T(1024)S(1)} %get-tuple-element.7, ...), kind=kOutput, calls=%fused_computation.10 | convolution fusion | flops 6486491136 | bytes 30433280 | tf_op jit(solution)/shard_map/rk,dk->rd/dot_general | solution.py:117
  329.1 86.9 %reduce-scatter.2.cloned.1.call-done = f32[128,4096]{1,0:T(8,128)} async-done(((f32[512,4096]{1,0:T(8,128)}), f32[128,4096]{1,0:T(8,128)}) %reduce-scatter.2.cloned.1.call-update) | async-done | bytes 2097168 | tf_op jit(solution)/shard_map/reduce_scatter | solution.py:116
  (77 shorter events, 43.5 us)
Async XLA Ops:
  7.2 58.0 %all-gather.4.cloned.1.call-start = ((), (), s32[]{:S(2)}) async-start(), calls=%async_computation.1 | async-start | bytes 5242880 | tf_op jit(solution)/shard_map/all_gather | solution.py:59
  7.9 408.1 %reduce-scatter.2.cloned.1.call-start = ((), (), s32[]{:S(2)}) async-start(), calls=%async_computation.2 | async-start | bytes 10485760 | tf_op jit(solution)/shard_map/reduce_scatter | solution.py:116
  9.8 17.3 %copy-start.9 = (f32[16,512]{0,1:T(8,128)}, f32[16,512]{0,1:T(8,128)S(1)}, u32[]{:S(2)}) copy-start(f32[16,512]{0,1:T(8,128)S(1)} %copy.28) | copy-start | bytes 98308
  77.7 35.0 %collective-permute-start = (bf16[2,1536]{1,0:T(2,128)(2,1)S(1)}, bf16[2,1536]{1,0:T(2,128)(2,1)S(1)}, u32[]{:S(2)}, u32[]{:S(2)}) collective-permute-start(bf16[2,1536]{1,0:T(2,128)(2,1)S(1)} %slice.97), channel_id=1, source_target_pairs={{0,4},{4,8},{8,12},{12,16},{16,20},{20,24},{24,28},{1,5},{5,9},{9,... | collective-permute-start | bytes 18440 | tf_op jit(solution)/shard_map/ppermute | solution.py:12
  113.2 1.0 copy-start.12
  131.2 9.5 %copy-start.1 = (f32[8,64,512]{1,0,2:T(8,128)S(1)}, f32[8,64,512]{1,0,2:T(8,128)}, u32[]{:S(2)}) copy-start(f32[8,64,512]{1,0,2:T(8,128)} %copy.32) | copy-start | bytes 3145732
  140.7 30.2 %copy-start = (f32[8,64,512]{1,0,2:T(8,128)S(1)}, f32[8,64,512]{1,0,2:T(8,128)}, u32[]{:S(2)}) copy-start(f32[8,64,512]{1,0,2:T(8,128)} %copy.38) | copy-start | bytes 3145732
  266.6 6.7 %copy-start.3 = (f32[16,512,9]{0,2,1:T(8,128)S(1)}, f32[16,512,9]{0,2,1:T(8,128)}, u32[]{:S(2)}) copy-start(f32[16,512,9]{0,2,1:T(8,128)} %copy.50) | copy-start | bytes 884740
  266.6 6.7 %copy-start.8 = (f32[512,8,64]{2,1,0:T(8,128)S(1)}, f32[512,8,64]{2,1,0:T(8,128)}, u32[]{:S(2)}) copy-start(f32[512,8,64]{2,1,0:T(8,128)} %fusion.2) | copy-start | bytes 3145732
  266.6 6.7 %copy-start.10 = (f32[16,512]{0,1:T(8,128)S(1)}, f32[16,512]{0,1:T(8,128)}, u32[]{:S(2)}) copy-start(f32[16,512]{0,1:T(8,128)} %copy-done.9) | copy-start | bytes 98308
  283.0 6.5 %copy-start.2 = (f32[16,512,9]{0,2,1:T(8,128)S(1)}, f32[16,512,9]{0,2,1:T(8,128)}, u32[]{:S(2)}) copy-start(f32[16,512,9]{0,2,1:T(8,128)} %copy.58) | copy-start | bytes 884740
  283.0 6.5 %copy-start.7 = (f32[512,8,64]{2,1,0:T(8,128)S(1)}, f32[512,8,64]{2,1,0:T(8,128)}, u32[]{:S(2)}) copy-start(f32[512,8,64]{2,1,0:T(8,128)} %fusion) | copy-start | bytes 3145732
  283.0 6.5 %copy-start.11 = (f32[16,512]{0,1:T(8,128)S(1)}, f32[16,512]{0,1:T(8,128)}, u32[]{:S(2)}) copy-start(f32[16,512]{0,1:T(8,128)} %copy-done.9) | copy-start | bytes 98308
  296.0 12.1 %copy-start.13 = (f32[512]{0:T(512)S(1)}, f32[512]{0:T(512)}, u32[]{:S(2)}) copy-start(f32[512]{0:T(512)} %param.12) | copy-start | bytes 6148
  312.2 3.3 copy-start.4
  312.2 3.3 copy-start.5
  312.2 3.3 copy-start.6
  312.4 3.1 collective-permute-start.1
Sparse Core Ops, SparseCore 0:
  9.8 55.2 all-gather.3
  329.2 86.7 reduce-scatter.1
where the time goes:
time: 433 us; the launch traced here: 426 us
  matrix products  130 us (30%)
  waiting for transfers between devices  127 us (29%)
  local copies, waits for them, and re-layouts  100 us (23%)
  blocking collectives  28.9 us (7%)
  other arithmetic  21.2 us (5%)
  between operations  14.6 us (3%)
    reduce_scatter x1, waiting for transfers between devices, shards(): lax.psum_scatter(jnp.einsum('rk,dk->rd', grad_streams, weight_cat, prefer...  86.9 us
    dot_general x2, matrix products, modal_block(): jnp.einsum('abc,kbc->kac', toeplitz, sections, precision=exact_mode)  60.7 us
    all_gather x1, waiting for transfers between devices, shards(): lax.all_gather(tokens, 'tp', axis=0, tiled=True)  38 us
    gather x2, local copies, waits for them, and re-layouts, modal_block(): filter_taps[jnp.maximum(lag_index, 0)]  33.1 us
    dot_general x2, matrix products, modal_block(): jnp.einsum('nbc,kbc->nkc', to_end, sections, precision=exact_mode)  17.8 us
    all_gather x1, blocking collectives, shards(): lax.all_gather(backward_sum[None], 'ctx', axis=0, tiled=True)  14.7 us
    all_gather x1, blocking collectives, shards(): lax.all_gather(forward_sum[None], 'ctx', axis=0, tiled=True)  14.2 us
    dot_general x1, matrix products, shards(): jnp.einsum('rk,dk->rd', grad_streams, weight_cat, preferred_element_type=...  13.3 us
  transfers between devices with their start and end apart: 4, of which 3 were waited for; matrix products, arithmetic and copies ran while one was open for 12% of the time, Pallas kernels for 0%

commit v1 on v0

--- a/solution.py
+++ b/solution.py
@@ -4,6 +4,9 @@
 from jax.sharding import PartitionSpec as P
 
 exact_mode = lax.Precision.HIGHEST
+rest_heaps_all = lambda x_part, mesh_dim: jnp.concatenate(
+    lax.all_to_all(jnp.stack(lax.axis_size(mesh_dim) * [x_part]), mesh_dim, 0, 0), axis=0
+)
 
 
 def from_behind(value, axis, steps):
@@ -56,9 +59,7 @@
     width = in_weight.shape[2]
     weight_cat = jnp.concatenate([in_weight[0], in_weight[1], in_weight[2]], axis=1)
     streams = jnp.dot(
-        lax.all_gather(tokens, "tp", axis=0, tiled=True),
-        weight_cat,
-        preferred_element_type=jnp.float32,
+        rest_heaps_all(tokens, "tp"), weight_cat, preferred_element_type=jnp.float32
     ).astype(jnp.bfloat16)
     length = streams.shape[0]
     tap_reach = short_taps.shape[1] - 1

time: 433 us -> 433 us (level)
  waiting for transfers between devices: 127 us -> 122 us
  starting transfers between devices: 3.11 us -> 8.08 us
    all_gather x1 -> x0, waiting for transfers between devices: 38 us -> none  [shards(): lax.all_gather(tokens, 'tp', axis=0, tiled=True)]
    all_to_all x0 -> x1, waiting for transfers between devices: none -> 33 us  [lax.all_to_all(jnp.stack(lax.axis_size(mesh_dim) * [x_part]), mesh_dim, 0...]
    all_to_all x0 -> x1, starting transfers between devices: none -> 5.32 us  [lax.all_to_all(jnp.stack(lax.axis_size(mesh_dim) * [x_part]), mesh_dim, 0...]
  transfers between devices with their start and end apart: 4 -> 4, of which waited for: 3 -> 3; matrix products, arithmetic and copies ran while one was open for 12% -> 11% of each run, Pallas kernels for 0% -> 0%
where the time goes in v1:
time: 433 us; the launch traced here: 426 us
  matrix products  130 us (30%)
  waiting for transfers between devices  122 us (28%)
  local copies, waits for them, and re-layouts  101 us (23%)
  blocking collectives  29.6 us (7%)
  other arithmetic  20.5 us (5%)
  between operations  14.6 us (3%)
  starting transfers between devices  8.08 us (2%)
    reduce_scatter x1, waiting for transfers between devices, shards(): lax.psum_scatter(jnp.einsum('rk,dk->rd', grad_streams, weight_cat, prefer...  86.9 us
    dot_general x2, matrix products, modal_block(): jnp.einsum('abc,kbc->kac', toeplitz, sections, precision=exact_mode)  60.7 us
    gather x2, local copies, waits for them, and re-layouts, modal_block(): filter_taps[jnp.maximum(lag_index, 0)]  33.1 us
    all_to_all x1, waiting for transfers between devices, lax.all_to_all(jnp.stack(lax.axis_size(mesh_dim) * [x_part]), mesh_dim, 0...  33 us
    dot_general x2, matrix products, modal_block(): jnp.einsum('nbc,kbc->nkc', to_end, sections, precision=exact_mode)  17.8 us
    all_gather x1, blocking collectives, shards(): lax.all_gather(backward_sum[None], 'ctx', axis=0, tiled=True)  15.4 us
    all_gather x1, blocking collectives, shards(): lax.all_gather(forward_sum[None], 'ctx', axis=0, tiled=True)  14.2 us
    dot_general x1, matrix products, shards(): jnp.einsum('rk,dk->rd', grad_streams, weight_cat, preferred_element_type=...  13.3 us
  transfers between devices with their start and end apart: 4, of which 3 were waited for; matrix products, arithmetic and copies ran while one was open for 11% of the time, Pallas kernels for 0%

profile of v1, /device:TPU:0, one launch (start us, length us, event | category | flops | bytes accessed | tf_op | source)
XLA Modules:
  0.0 426.0 jit_solution(2319887598778068317)
XLA Ops:
  10.9 5.3 %all-to-all-start = ((bf16[4,128,4096]{2,1,0:T(8,128)(2,1)}), bf16[4,128,4096]{2,1,0:T(8,128)(2,1)}, u32[]{:S(2)}, u32[]{:S(2)}) async-start(bf16[4,128,4096]{2,1,0:T(8,128)(2,1)} %stack.2), calls=%async_computation | async-start | bytes 8388608 | tf_op jit(solution)/shard_map/all_to_all | solution.py:8
  16.9 6.0 %multiply_reduce_fusion = f32[64,512]{0,1:T(8,128)S(1)} fusion(f32[16,512]{0,1:T(8,128)S(1)} %copy.29, f32[16,512]{0,1:T(8,128)S(1)} %copy.28), kind=kLoop, calls=%fused_computation.20 | loop fusion | flops 1540096 | bytes 196608 | tf_op jit(solution)/shard_map/reduce_sum | solution.py:25
  22.8 9.0 %slice_bitcast_fusion.2 = (bf16[4096,512]{1,0:T(8,128)(2,1)}, bf16[4096,512]{1,0:T(8,128)(2,1)}, bf16[4096,512]{1,0:T(8,128)(2,1)}) fusion(bf16[3,4096,512]{2,1,0:T(8,128)(2,1)} %param.8), kind=kLoop, calls=%fused_computation.23 | loop fusion | bytes 25165824 | tf_op jit(solution)/shard_map/squeeze | solution.py:60
  31.9 33.0 %all-to-all-done = bf16[4,128,4096]{2,1,0:T(8,128)(2,1)} async-done(((bf16[4,128,4096]{2,1,0:T(8,128)(2,1)}), bf16[4,128,4096]{2,1,0:T(8,128)(2,1)}, u32[]{:S(2)}, u32[]{:S(2)}) %all-to-all-start) | async-done | bytes 4194336 | tf_op jit(solution)/shard_map/all_to_all | solution.py:8
  64.8 12.5 %fusion.22 = bf16[512,1536]{1,0:T(8,128)(2,1)S(1)} fusion(bf16[512,4096]{1,0:T(8,128)(2,1)} %bitcast.10, bf16[4096,512]{1,0:T(8,128)(2,1)} %get-tuple-element.10, bf16[4096,512]{1,0:T(8,128)(2,1)} %get-tuple-element.11, bf16[4096,512]{1,0:T(8,128)(2,1)} %get-tuple-element.9), kind=kOutput, calls=%fused_computation.37 | convolution fusion | flops 6480986112 | bytes 18350080 | tf_op jit(solution)/shard_map/dot_general | solution.py:61
  78.9 16.8 %gather_fusion = f32[4096,512]{1,0:T(8,128)} fusion(f32[64,512]{1,0:T(8,128)S(1)} %copy.30, s32[4096]{0:T(1024)S(1)} %broadcast_clamp_fusion), kind=kCustom, calls=%fused_computation | custom fusion | bytes 16793600 | tf_op jit(solution)/shard_map/gather | solution.py:27
  95.7 16.3 %copy.31 = f32[64,64,512]{1,0,2:T(8,128)} copy(f32[64,64,512]{2,1,0:T(8,128)} %bitcast.52) | data formatting | bytes 16777216 | tf_op jit(solution)/shard_map/gather | solution.py:27
  115.4 8.9 %rev.6 = f32[512,512]{1,0:T(8,128)} reverse(f32[512,512]{1,0:T(8,128)} %get-tuple-element.15), dimensions={0} | reverse | bytes 2097152 | tf_op jit(solution)/shard_map/rev | solution.py:83
  130.7 9.5 %fusion.43 = f32[16,512,8]{0,2,1:T(8,128)} fusion(f32[8,64,512]{1,0,2:T(8,128)} %copy.32, f32[64]{0:T(128)S(1)} %iota_subtract_fusion.2, f32[16,512]{0,1:T(8,128)S(1)} %copy.29), kind=kOutput, calls=%fused_computation.64 | convolution fusion | flops 50855936 | bytes 1343744 | tf_op jit(solution)/shard_map/nbc,kbc->nkc/dot_general | solution.py:30
  140.1 30.2 %fusion.2 = f32[512,8,64]{2,1,0:T(8,128)} fusion(f32[8,64,512]{1,0,2:T(8,128)S(1)} %copy-done.1, f32[64,64,512]{1,0,2:T(8,128)} %copy.31, pred[64,64]{1,0:T(8,128)(4,1)S(1)} %subtract_compare_fusion), kind=kOutput, calls=%fused_computation.3 | convolution fusion | flops 203423744 | bytes 10489856 | tf_op jit(solution)/shard_map/abc,kbc->kac/dot_general | solution.py:28
  170.3 30.5 %fusion = f32[512,8,64]{2,1,0:T(8,128)} fusion(f32[8,64,512]{1,0,2:T(8,128)S(1)} %copy-done, f32[64,64,512]{1,0,2:T(8,128)} %copy.31, pred[64,64]{1,0:T(8,128)(4,1)S(1)} %subtract_compare_fusion), kind=kOutput, calls=%fused_computation.1 | convolution fusion | flops 203423744 | bytes 10489856 | tf_op jit(solution)/shard_map/abc,kbc->kac/dot_general | solution.py:28
  200.9 8.3 %fusion.44 = f32[16,512,8]{0,2,1:T(8,128)} fusion(f32[8,64,512]{1,0,2:T(8,128)S(1)} %copy-done, f32[64]{0:T(128)S(1)} %iota_subtract_fusion.2, f32[16,512]{0,1:T(8,128)S(1)} %copy.29), kind=kOutput, calls=%fused_computation.65 | convolution fusion | flops 50855936 | bytes 1343744 | tf_op jit(solution)/shard_map/nbc,kbc->nkc/dot_general | solution.py:30
  217.7 4.5 %copy.58 = f32[16,512,9]{0,2,1:T(8,128)} copy(f32[16,512,9]{1,0,2:T(8,128)} %get-tuple-element.2) | data formatting | bytes 589824 | tf_op jit(solution)/shard_map/kmnc,nmc->nkc/dot_general | solution.py:36
  225.7 15.4 %all-gather.1 = f32[128,1,512]{2,1,0:T(1,128)S(1)} all-gather(f32[16,1,512]{2,1,0:T(1,128)S(1)} %copy.40), channel_id=3, replica_groups=mesh['ctx'=8,'tp'=4] {'ctx'}, dimensions={0}, use_global_device_ids=true | all-gather | bytes 294912 | tf_op jit(solution)/shard_map/all_gather | solution.py:87
  241.8 4.5 %copy.50 = f32[16,512,9]{0,2,1:T(8,128)} copy(f32[16,512,9]{1,0,2:T(8,128)} %get-tuple-element.3) | data formatting | bytes 589824 | tf_op jit(solution)/shard_map/kmnc,nmc->nkc/dot_general | solution.py:36
  249.8 14.2 %all-gather = f32[128,1,512]{2,1,0:T(1,128)S(1)} all-gather(f32[16,1,512]{2,1,0:T(1,128)S(1)} %copy.34), channel_id=2, replica_groups=mesh['ctx'=8,'tp'=4] {'ctx'}, dimensions={0}, use_global_device_ids=true | all-gather | bytes 294912 | tf_op jit(solution)/shard_map/all_gather | solution.py:86
  266.9 6.7 %fusion.12 = f32[512,8,64]{2,1,0:T(8,128)S(1)} fusion(f32[64]{0:T(128)S(1)} %iota_add_fusion, f32[16,512]{0,1:T(8,128)S(1)} %copy.29, f32[16,512]{0,1:T(8,128)} %copy-done.9, f32[8]{0:T(128)S(1)} %multiply_convert_fusion.3, f32[16,512]{0,1:T(8,128)} %copy.35), kind=kOutput, calls=%fused_computation.15 | convolution fusion | flops 51511296 | bytes 1147168 | tf_op jit(solution)/shard_map/nac,nkc->kac/dot_general | solution.py:54
  273.6 6.5 %add_bitcast_fusion.1 = f32[8,64,512]{1,0,2:T(8,128)} fusion(f32[512,8,64]{2,1,0:T(8,128)S(1)} %fusion.12, f32[512,8,64]{2,1,0:T(8,128)S(1)} %copy-done.8, f32[64]{0:T(128)S(1)} %iota_add_fusion, f32[16,512]{0,1:T(8,128)S(1)} %copy.29, f32[16,512]{0,1:T(8,128)S(1)} %copy-done.10, f32[16,9,512]{0,1,2:T(8,128)S(1)} %bitcast.56), kind=kOutput, calls=%fused_computation.45 | convolution fusion | flops 51904512 | bytes 7864832 | tf_op jit(solution)/shard_map/nac,nkc->kac/dot_general | solution.py:38
  283.2 6.5 %fusion.10 = f32[512,8,64]{2,1,0:T(8,128)S(1)} fusion(f32[64]{0:T(128)S(1)} %iota_add_fusion, f32[16,512]{0,1:T(8,128)S(1)} %copy.29, f32[16,512]{0,1:T(8,128)} %copy-done.9, f32[16,512]{0,1:T(8,128)} %copy.41, f32[8]{0:T(128)S(1)} %multiply_convert_fusion.3), kind=kOutput, calls=%fused_computation.13 | convolution fusion | flops 51511296 | bytes 1147168 | tf_op jit(solution)/shard_map/nac,nkc->kac/dot_general | solution.py:54
  289.8 6.5 %add_bitcast_fusion = f32[8,64,512]{1,0,2:T(8,128)} fusion(f32[512,8,64]{2,1,0:T(8,128)S(1)} %fusion.10, f32[512,8,64]{2,1,0:T(8,128)S(1)} %copy-done.7, f32[64]{0:T(128)S(1)} %iota_add_fusion, f32[16,512]{0,1:T(8,128)S(1)} %copy.29, f32[16,512]{0,1:T(8,128)S(1)} %copy-done.11, f32[16,9,512]{0,1,2:T(8,128)S(1)} %bitcast.54), kind=kOutput, calls=%fused_computation.43 | convolution fusion | flops 51904512 | bytes 7864832 | tf_op jit(solution)/shard_map/nac,nkc->kac/dot_general | solution.py:38
  299.5 8.9 %rev.7 = f32[512,512]{1,0:T(8,128)} reverse(f32[512,512]{1,0:T(8,128)} %bitcast.58), dimensions={0} | reverse | bytes 2097152 | tf_op jit(solution)/shard_map/rev | solution.py:103
  308.4 4.1 slice_multiply_fusion.5
  316.0 13.3 %fusion.8 = f32[512,4096]{1,0:T(8,128)} fusion(bf16[4096,512]{1,0:T(8,128)(2,1)} %get-tuple-element.10, bf16[4096,512]{1,0:T(8,128)(2,1)} %get-tuple-element.11, bf16[4096,512]{1,0:T(8,128)(2,1)} %get-tuple-element.9, f32[514,1536]{1,0:T(8,128)S(1)} %pad_maximum_fusion.3, f32[1536]{0:T(1024)S(1)} %get-tuple-element.8, f32[1536]{0:T(1024)S(1)} %get-tuple-element.7, ...), kind=kOutput, calls=%fused_computation.10 | convolution fusion | flops 6486491136 | bytes 30433280 | tf_op jit(solution)/shard_map/rk,dk->rd/dot_general | solution.py:118
  329.3 86.9 %reduce-scatter.2.cloned.1.call-done = f32[128,4096]{1,0:T(8,128)} async-done(((f32[512,4096]{1,0:T(8,128)}), f32[128,4096]{1,0:T(8,128)}) %reduce-scatter.2.cloned.1.call-update) | async-done | bytes 2097168 | tf_op jit(solution)/shard_map/reduce_scatter | solution.py:117
  (83 shorter events, 47.2 us)
Async XLA Ops:
  10.9 5.4 %copy-start.14 = (f32[16,512]{1,0:T(8,128)S(1)}, f32[16,512]{1,0:T(8,128)}, u32[]{:S(2)}) copy-start(f32[16,512]{1,0:T(8,128)} %param.10) | copy-start | bytes 98308
  10.9 5.6 %copy-start.13 = (f32[16,512]{1,0:T(8,128)S(1)}, f32[16,512]{1,0:T(8,128)}, u32[]{:S(2)}) copy-start(f32[16,512]{1,0:T(8,128)} %param.11) | copy-start | bytes 98308
  10.9 6.0 %copy-start.15 = (f32[3,3,512]{2,1,0:T(4,128)S(1)}, f32[3,3,512]{2,1,0:T(4,128)}, u32[]{:S(2)}) copy-start(f32[3,3,512]{2,1,0:T(4,128)} %param.9) | copy-start | bytes 55300
  10.9 54.0 %all-to-all-start = ((bf16[4,128,4096]{2,1,0:T(8,128)(2,1)}), bf16[4,128,4096]{2,1,0:T(8,128)(2,1)}, u32[]{:S(2)}, u32[]{:S(2)}) async-start(bf16[4,128,4096]{2,1,0:T(8,128)(2,1)} %stack.2), calls=%async_computation | async-start | bytes 8388608 | tf_op jit(solution)/shard_map/all_to_all | solution.py:8
  16.2 400.1 %reduce-scatter.2.cloned.1.call-start = ((), (), s32[]{:S(2)}) async-start(), calls=%async_computation.2 | async-start | bytes 10485760 | tf_op jit(solution)/shard_map/reduce_scatter | solution.py:117
  16.6 15.3 %copy-start.9 = (f32[16,512]{0,1:T(8,128)}, f32[16,512]{0,1:T(8,128)S(1)}, u32[]{:S(2)}) copy-start(f32[16,512]{0,1:T(8,128)S(1)} %copy.28) | copy-start | bytes 98308
  77.3 34.7 %collective-permute-start = (bf16[2,1536]{1,0:T(2,128)(2,1)S(1)}, bf16[2,1536]{1,0:T(2,128)(2,1)S(1)}, u32[]{:S(2)}, u32[]{:S(2)}) collective-permute-start(bf16[2,1536]{1,0:T(2,128)(2,1)S(1)} %slice.97), channel_id=1, source_target_pairs={{0,4},{4,8},{8,12},{12,16},{16,20},{20,24},{24,28},{1,5},{5,9},{9,... | collective-permute-start | bytes 18440 | tf_op jit(solution)/shard_map/ppermute | solution.py:15
  112.6 1.0 copy-start.12
  130.7 9.5 %copy-start.1 = (f32[8,64,512]{1,0,2:T(8,128)S(1)}, f32[8,64,512]{1,0,2:T(8,128)}, u32[]{:S(2)}) copy-start(f32[8,64,512]{1,0,2:T(8,128)} %copy.32) | copy-start | bytes 3145732
  140.1 30.2 %copy-start = (f32[8,64,512]{1,0,2:T(8,128)S(1)}, f32[8,64,512]{1,0,2:T(8,128)}, u32[]{:S(2)}) copy-start(f32[8,64,512]{1,0,2:T(8,128)} %copy.38) | copy-start | bytes 3145732
  266.9 6.7 %copy-start.3 = (f32[16,512,9]{0,2,1:T(8,128)S(1)}, f32[16,512,9]{0,2,1:T(8,128)}, u32[]{:S(2)}) copy-start(f32[16,512,9]{0,2,1:T(8,128)} %copy.50) | copy-start | bytes 884740
  266.9 6.7 %copy-start.8 = (f32[512,8,64]{2,1,0:T(8,128)S(1)}, f32[512,8,64]{2,1,0:T(8,128)}, u32[]{:S(2)}) copy-start(f32[512,8,64]{2,1,0:T(8,128)} %fusion.2) | copy-start | bytes 3145732
  266.9 6.7 %copy-start.10 = (f32[16,512]{0,1:T(8,128)S(1)}, f32[16,512]{0,1:T(8,128)}, u32[]{:S(2)}) copy-start(f32[16,512]{0,1:T(8,128)} %copy-done.9) | copy-start | bytes 98308
  283.2 6.5 %copy-start.2 = (f32[16,512,9]{0,2,1:T(8,128)S(1)}, f32[16,512,9]{0,2,1:T(8,128)}, u32[]{:S(2)}) copy-start(f32[16,512,9]{0,2,1:T(8,128)} %copy.58) | copy-start | bytes 884740
  283.2 6.5 %copy-start.7 = (f32[512,8,64]{2,1,0:T(8,128)S(1)}, f32[512,8,64]{2,1,0:T(8,128)}, u32[]{:S(2)}) copy-start(f32[512,8,64]{2,1,0:T(8,128)} %fusion) | copy-start | bytes 3145732
  283.2 6.5 %copy-start.11 = (f32[16,512]{0,1:T(8,128)S(1)}, f32[16,512]{0,1:T(8,128)}, u32[]{:S(2)}) copy-start(f32[16,512]{0,1:T(8,128)} %copy-done.9) | copy-start | bytes 98308
  296.3 12.1 %copy-start.16 = (f32[512]{0:T(512)S(1)}, f32[512]{0:T(512)}, u32[]{:S(2)}) copy-start(f32[512]{0:T(512)} %param.12) | copy-start | bytes 6148
  312.5 3.3 copy-start.4
  312.5 3.3 copy-start.5
  312.5 3.3 copy-start.6
  312.7 3.1 collective-permute-start.1
Sparse Core Ops, SparseCore 0:
  329.4 86.7 reduce-scatter.1
